TPU v7x, 32 devices: a whole 2x2x4 slice. The times are simulated.
32 devices in a mesh: gx: 8 (over z, core), gy: 4 (over y, x).
Axes of the slice: x: 2, y: 2, z: 4, core: 2. Of those that a mesh axis runs over, the one named last changes fastest.
Arguments:
- base_state: float32 [3, 32, 32, 128], P(None, 'gx', 'gy'), may hold values from -5 to 5
- adjoint_block: float32 [32, 3, 32, 32, 128], P(None, None, 'gx', 'gy'), may hold values from -2500 to 2500
Outputs:
- q_block: float32 [32, 3, 32, 32, 128], P(None, None, 'gx', 'gy')
- r_factor: float32 [32, 32], replicated
All inputs are finite; a program needn't handle non-finite values.
Results may differ from a plain program's by a relative error of at most 0.00015.
Values sent between devices are 32-bit elements; how exact they have to be, the bound alone decides.
A program may use at most 64 MiB of HBM per device.

v0:
```python
import math
import jax
import jax.numpy as jnp
from jax import lax
from jax.sharding import PartitionSpec as P

ADVECT = 0.1
DIFFUSE = 0.08
DRIVE_SCALE = 0.25
WAVENUMBER = 4.0


def with_halo(value, sides, width):
    for axis, dim in sides:
        devices, length = (lax.axis_size(axis), value.shape[dim])
        up = [(i, (i + 1) % devices) for i in range(devices)]
        down = [(j, i) for i, j in up]
        last = lax.slice_in_dim(value, length - width, length, axis=dim)
        first = lax.slice_in_dim(value, 0, width, axis=dim)
        before = lax.ppermute(last, axis, up)
        after = lax.ppermute(first, axis, down)
        value = jnp.concatenate([before, value, after], axis=dim)
    return value


def advance(padded, column_index, ny_total):
    centre = padded[:, 1:-1, 1:-1, :]
    eastern = padded[:, 2:, 1:-1, :]
    western = padded[:, :-2, 1:-1, :]
    northern = padded[:, 1:-1, 2:, :]
    southern = padded[:, 1:-1, :-2, :]
    upward = jnp.roll(centre, -1, axis=3)
    downward = jnp.roll(centre, 1, axis=3)
    laplacian = eastern + western + northern + southern + upward + downward - 6.0 * centre
    advection = (
        centre[0:1] * (eastern - western)
        + centre[1:2] * (northern - southern)
        + centre[2:3] * (upward - downward)
    )
    phases = 2.0 * math.pi * WAVENUMBER * column_index.astype(jnp.float32) / float(ny_total)
    forcing = DRIVE_SCALE * jnp.sin(phases)
    nothing = jnp.zeros_like(forcing)
    driven = jnp.stack([forcing, nothing, nothing])[:, None, :, None]
    return centre + DIFFUSE * laplacian - ADVECT * advection + driven


def adjoint(base_ext, block_ext):
    inner = block_ext[:, :, 1:-1, 1:-1, :]
    base_inner = base_ext[:, 1:-1, 1:-1, :]
    base_east = base_ext[:, 2:, 1:-1, :]
    base_west = base_ext[:, :-2, 1:-1, :]
    base_north = base_ext[:, 1:-1, 2:, :]
    base_south = base_ext[:, 1:-1, :-2, :]
    block_east = block_ext[:, :, 2:, 1:-1, :]
    block_west = block_ext[:, :, :-2, 1:-1, :]
    block_north = block_ext[:, :, 1:-1, 2:, :]
    block_south = block_ext[:, :, 1:-1, :-2, :]
    carried = base_inner[2] * inner
    flux = base_east[0] * block_east - base_west[0] * block_west
    flux = flux + base_north[1] * block_north - base_south[1] * block_south
    flux = flux + jnp.roll(carried, -1, axis=-1) - jnp.roll(carried, 1, axis=-1)
    grad_x = base_east - base_west
    grad_y = base_north - base_south
    grad_z = jnp.roll(base_inner, -1, axis=3) - jnp.roll(base_inner, 1, axis=3)
    coupling = jnp.stack(
        [
            jnp.sum(inner * grad_x, axis=1),
            jnp.sum(inner * grad_y, axis=1),
            jnp.sum(inner * grad_z, axis=1),
        ],
        axis=1,
    )
    laplacian = (
        block_east
        + block_west
        + block_north
        + block_south
        + jnp.roll(inner, -1, axis=-1)
        + jnp.roll(inner, 1, axis=-1)
        - 6.0 * inner
    )
    return inner + ADVECT * (flux - coupling) + DIFFUSE * laplacian


def on_device(base_state, adjoint_block):
    vectors = adjoint_block.shape[0]
    width_y = base_state.shape[2]
    ny_total = width_y * lax.axis_size("gy")
    offset = lax.axis_index("gy") * width_y
    padded = with_halo(base_state, (("gx", 1), ("gy", 2)), 2)
    column_index = (offset + jnp.arange(-1, width_y + 1, dtype=jnp.int32)) % ny_total
    base_ext = advance(padded, column_index, ny_total)
    block_ext = with_halo(adjoint_block, (("gx", 2), ("gy", 3)), 1)
    updated = adjoint(base_ext, block_ext)
    flat = updated.reshape(vectors, -1)
    partial_gram = jnp.dot(
        flat, flat.T, precision=lax.Precision.HIGHEST, preferred_element_type=jnp.float32
    )
    entries = flat.shape[1] * lax.axis_size("gx") * lax.axis_size("gy")
    gram = lax.psum(partial_gram, ("gx", "gy")) / float(entries)
    lower = jnp.linalg.cholesky(gram)
    inverse = lax.linalg.triangular_solve(
        lower, jnp.eye(vectors, dtype=jnp.float32), left_side=True, lower=True
    )
    q_block = jnp.dot(
        inverse, flat, precision=lax.Precision.HIGHEST, preferred_element_type=jnp.float32
    ).reshape(updated.shape)
    return (q_block, lower.T)


def solution(mesh):
    in_specs = (P(None, "gx", "gy", None), P(None, None, "gx", "gy", None))
    out_specs = (P(None, None, "gx", "gy", None), P())
    return jax.shard_map(
        on_device, mesh=mesh, in_specs=in_specs, out_specs=out_specs, check_vma=False
    )
```

profile of v0, /device:TPU:0, one launch (start us, length us, event | category | flops | bytes accessed | tf_op | source)
XLA Modules:
  0.0 99.8 jit_solution(14381790056354557528)
XLA Ops:
  0.6 1.5 %fusion.34 = (f32[3,2,8,128]{3,2,1,0:T(8,128)}, f32[3,2,8,128]{3,2,1,0:T(8,128)}) fusion(f32[3,4,8,128]{3,2,1,0:T(8,128)} %param.2), kind=kLoop, calls=%fused_computation.78 | loop fusion | bytes 98304 | tf_op jit(solution)/shard_map/slice | solution.py:19
  2.1 4.5 %collective-permute-start.1 = (f32[3,2,8,128]{3,2,1,0:T(8,128)}, f32[3,2,8,128]{3,2,1,0:T(8,128)}, u32[]{:S(2)}, u32[]{:S(2)}) collective-permute-start(f32[3,2,8,128]{3,2,1,0:T(8,128)} %get-tuple-element.49), channel_id=1, source_target_pairs={{4,0},{8,4},{12,8},{16,12},{20,16},{24,20},{28,24},{0,28},{5,1},{9... | collective-permute-start | bytes 73736 | tf_op jit(solution)/shard_map/ppermute | solution.py:21
  6.7 2.1 %fusion.24 = (f32[32,3,1,8,128]{4,3,2,0,1:T(8,128)}, f32[32,3,1,8,128]{4,3,2,0,1:T(8,128)}) fusion(f32[32,3,4,8,128]{4,3,2,1,0:T(8,128)} %param.3), kind=kLoop, calls=%fused_computation.68 | loop fusion | bytes 1572864 | tf_op jit(solution)/shard_map/slice | solution.py:19
  8.7 3.5 %collective-permute-start.4 = (f32[32,3,1,8,128]{4,3,2,0,1:T(8,128)}, f32[32,3,1,8,128]{4,3,2,0,1:T(8,128)S(1)}, u32[]{:S(2)}, u32[]{:S(2)}) collective-permute-start(f32[32,3,1,8,128]{4,3,2,0,1:T(8,128)} %get-tuple-element.17), channel_id=1, source_target_pairs={{4,0},{8,4},{12,8},{16,12},{20,16},{24,20},{28,24},{0,28},{5,1},{9... | collective-permute-start | bytes 1179656 | tf_op jit(solution)/shard_map/ppermute | solution.py:21
  12.3 1.7 %fusion.25 = (f32[32,3,4,8,1]{4,3,2,0,1:T(8,128)S(1)}, f32[32,3,4,8,1]{4,3,2,0,1:T(8,128)}) fusion(f32[32,3,4,8,128]{4,3,2,1,0:T(8,128)S(1)} %copy-done), kind=kLoop, calls=%fused_computation.69 | loop fusion | bytes 3170304 | tf_op jit(solution)/shard_map/jit(_roll_static)/slice | solution.py:79
  14.0 2.2 %fusion.26 = (f32[32,3,4,8,127]{4,3,2,0,1:T(8,128)}, f32[32,3,4,8,127]{4,3,2,0,1:T(8,128)}) fusion(f32[32,3,4,8,128]{4,3,2,1,0:T(8,128)S(1)} %copy-done), kind=kLoop, calls=%fused_computation.70 | loop fusion | bytes 6266880 | tf_op jit(solution)/shard_map/jit(_roll_static)/slice | solution.py:79
  16.2 0.7 constant_dynamic-update-slice_fusion.2
  16.9 0.8 constant_dynamic-update-slice_fusion.1
  17.8 0.7 constant_dynamic-update-slice_fusion
  18.5 1.5 %collective-permute-start.2 = (f32[3,8,2,128]{3,2,1,0:T(2,128)S(1)}, f32[3,8,2,128]{3,2,1,0:T(2,128)S(1)}, u32[]{:S(2)}, u32[]{:S(2)}) collective-permute-start(f32[3,8,2,128]{3,2,1,0:T(2,128)S(1)} %get-tuple-element.47), channel_id=1, source_target_pairs={{0,1},{1,2},{2,3},{3,0},{4,5},{5,6},{6,7},{7,4},{8,9},{9,10},{10,1... | collective-permute-start | bytes 73736 | tf_op jit(solution)/shard_map/ppermute | solution.py:20
  20.1 1.4 %collective-permute-start.3 = (f32[3,8,2,128]{3,2,1,0:T(2,128)S(1)}, f32[3,8,2,128]{3,2,1,0:T(2,128)S(1)}, u32[]{:S(2)}, u32[]{:S(2)}) collective-permute-start(f32[3,8,2,128]{3,2,1,0:T(2,128)S(1)} %get-tuple-element.48), channel_id=1, source_target_pairs={{1,0},{2,1},{3,2},{0,3},{5,4},{6,5},{7,6},{4,7},{9,8},{10,9},{11,1... | collective-permute-start | bytes 73736 | tf_op jit(solution)/shard_map/ppermute | solution.py:21
  21.5 0.1 fusion.21
  21.5 0.1 copy.62
  21.7 1.6 %collective-permute-done.2 = f32[3,8,2,128]{3,2,1,0:T(2,128)S(1)} collective-permute-done((f32[3,8,2,128]{3,2,1,0:T(2,128)S(1)}, f32[3,8,2,128]{3,2,1,0:T(2,128)S(1)}, u32[]{:S(2)}, u32[]{:S(2)}) %collective-permute-start.2) | collective-permute-done | bytes 24608 | tf_op jit(solution)/shard_map/ppermute | solution.py:20
  23.3 0.6 collective-permute-done.3
  24.0 0.1 fusion.29
  24.1 0.1 fusion.30
  24.2 0.2 subtract_add_fusion
  24.4 0.1 fusion.31
  24.5 0.1 fusion.32
  24.5 0.1 slice_subtract_fusion
  24.6 0.5 multiply_reduce_fusion.2
  25.2 1.0 %constant_dynamic-update-slice_fusion.5 = f32[32,3,6,8,128]{4,3,2,0,1:T(8,128)S(1)} fusion(f32[32,3,1,8,128]{4,3,2,0,1:T(8,128)} %collective-permute-done.5), kind=kLoop, calls=%fused_computation.55 | loop fusion | bytes 786432
  26.2 0.3 constant_dynamic-update-slice_fusion.4
  26.6 0.4 fusion.23
  27.1 2.4 %collective-permute-start.7 = (f32[32,3,6,1,128]{4,0,3,2,1:T(8,128)S(1)}, f32[32,3,6,1,128]{4,0,3,2,1:T(8,128)S(1)}, u32[]{:S(2)}, u32[]{:S(2)}) collective-permute-start(f32[32,3,6,1,128]{4,0,3,2,1:T(8,128)S(1)} %copy.59), channel_id=1, source_target_pairs={{0,1},{1,2},{2,3},{3,0},{4,5},{5,6},{6,7},{7,4},{8,9},{9,10},{10,1... | collective-permute-start | bytes 884744 | tf_op jit(solution)/shard_map/ppermute | solution.py:20
  29.5 0.5 collective-permute-start.6
  30.0 0.6 fusion.28
  30.6 0.6 fusion.27
  31.2 4.8 %collective-permute-done.7 = f32[32,3,6,1,128]{4,0,3,2,1:T(8,128)S(1)} collective-permute-done((f32[32,3,6,1,128]{4,0,3,2,1:T(8,128)S(1)}, f32[32,3,6,1,128]{4,0,3,2,1:T(8,128)S(1)}, u32[]{:S(2)}, u32[]{:S(2)}) %collective-permute-start.7) | collective-permute-done | bytes 294944 | tf_op jit(solution)/shard_map/ppermute | solution.py:20
  36.0 0.3 copy.60
  36.3 2.9 %collective-permute-done.6 = f32[32,3,6,1,128]{4,0,3,2,1:T(8,128)S(1)} collective-permute-done((f32[32,3,6,1,128]{4,0,3,2,1:T(8,128)S(1)}, f32[32,3,6,1,128]{4,0,3,2,1:T(8,128)S(1)}, u32[]{:S(2)}, u32[]{:S(2)}) %collective-permute-start.6) | collective-permute-done | bytes 294944 | tf_op jit(solution)/shard_map/ppermute | solution.py:21
  39.2 0.3 copy.58
  39.6 3.9 %fusion.4 = f32[32,3,4,8,128]{4,3,2,0,1:T(8,128)S(1)} fusion(f32[32,3,4,8,128]{4,3,2,0,1:T(8,128)S(1)} %copy.62, f32[32,3,4,8,1]{4,3,2,0,1:T(8,128)S(1)} %get-tuple-element.26, f32[32,3,4,8,127]{4,3,2,0,1:T(8,128)S(1)} %get-tuple-element.28, f32[32,3,4,8,127]{4,3,2,0,1:T(8,128)S(1)} %get-tuple-element.27, f32[32,3,4,8,1]{4,3,2,0,1:T(8,128)S(1)} %get-tuple-element.25, ...), kind=kLoop, calls=%fused_computation.10 | loop fusion | flops 12189696 | bytes 14811136 | tf_op jit(solution)/shard_map/add | solution.py:82
  43.5 2.2 %fusion.12 = f32[32,32]{0,1:T(8,128)S(1)} fusion(f32[32,3,4,8,128]{4,3,2,0,1:T(8,128)S(1)} %fusion.4), kind=kOutput, calls=%fused_computation.22 | convolution fusion | flops 150994944 | bytes 1576960 | tf_op jit(solution)/shard_map/dot_general | solution.py:96
  45.6 0.1 copy.72
  45.8 40.7 %psum.7 = f32[32,32]{0,1:T(8,128)S(1)} all-reduce(f32[32,32]{0,1:T(8,128)S(1)} %fusion.12), channel_id=1, replica_groups=mesh['gx'=8,'gy'=4] {'gx','gy'}, use_global_device_ids=true, to_apply=%region_3.4 | all-reduce | flops 1024 | bytes 8192 | tf_op jit(solution)/shard_map/psum | solution.py:100
  86.5 0.9 copy.96
  87.4 0.3 copy.80
  87.7 0.1 copy.71
  87.8 2.9 %cholesky.17 = f32[32,32]{1,0:T(8,128)S(1)} custom-call(f32[32,32]{1,0:T(8,128)S(1)} %fusion.16), custom_call_target="Cholesky" | custom-call | tf_op jit(solution)/shard_map/jit(cholesky)/cholesky | solution.py:101
  90.8 0.6 compare_reduce_fusion
  91.4 0.7 fusion.17
  92.1 0.7 copy.75
  92.7 2.4 %custom-call.6 = f32[1,32,32]{1,2,0:T(8,128)S(1)} custom-call(f32[1,32,32]{2,1,0:T(8,128)S(1)} %get-tuple-element.52), custom_call_target="InvertDiagBlocksLowerTriangular" | custom-call | tf_op jit(solution)/shard_map/triangular_solve | solution.py:102
  95.2 0.2 convolution_bitcast_fusion
  95.4 2.3 %fusion.8 = f32[32,3,4,8,128]{4,0,3,2,1:T(8,128)S(1)} fusion(f32[32,32,1,1,1]{1,0,4,3,2:T(8,128)S(1)} %convolution_bitcast_fusion, f32[3,4,8,128,32]{3,2,1,0,4:T(8,128)S(1)} %bitcast.50), kind=kOutput, calls=%fused_computation.15 | convolution fusion | flops 150994944 | bytes 3149824 | tf_op jit(solution)/shard_map/dot_general | solution.py:105
  97.7 2.1 %copy.74 = f32[32,3,4,8,128]{4,3,2,1,0:T(8,128)} copy(f32[32,3,4,8,128]{4,0,3,2,1:T(8,128)S(1)} %fusion.8) | data formatting | bytes 3145728
  (25 shorter events, 0.3 us)
Async XLA Ops:
  0.6 11.6 %copy-start = (f32[32,3,4,8,128]{4,3,2,1,0:T(8,128)S(1)}, f32[32,3,4,8,128]{4,3,2,1,0:T(8,128)}, u32[]{:S(2)}) copy-start(f32[32,3,4,8,128]{4,3,2,1,0:T(8,128)} %param.3) | copy-start | bytes 4718596
  2.1 15.6 %collective-permute-start.1 = (f32[3,2,8,128]{3,2,1,0:T(8,128)}, f32[3,2,8,128]{3,2,1,0:T(8,128)}, u32[]{:S(2)}, u32[]{:S(2)}) collective-permute-start(f32[3,2,8,128]{3,2,1,0:T(8,128)} %get-tuple-element.49), channel_id=1, source_target_pairs={{4,0},{8,4},{12,8},{16,12},{20,16},{24,20},{28,24},{0,28},{5,1},{9... | collective-permute-start | bytes 73736 | tf_op jit(solution)/shard_map/ppermute | solution.py:21
  6.7 9.6 %collective-permute-start = (f32[3,2,8,128]{3,2,1,0:T(8,128)}, f32[3,2,8,128]{3,2,1,0:T(8,128)}, u32[]{:S(2)}, u32[]{:S(2)}) collective-permute-start(f32[3,2,8,128]{3,2,1,0:T(8,128)} %get-tuple-element.50), channel_id=1, source_target_pairs={{0,4},{4,8},{8,12},{12,16},{16,20},{20,24},{24,28},{28,0},{1,5},{5... | collective-permute-start | bytes 73736 | tf_op jit(solution)/shard_map/ppermute | solution.py:20
  8.7 17.9 %collective-permute-start.4 = (f32[32,3,1,8,128]{4,3,2,0,1:T(8,128)}, f32[32,3,1,8,128]{4,3,2,0,1:T(8,128)S(1)}, u32[]{:S(2)}, u32[]{:S(2)}) collective-permute-start(f32[32,3,1,8,128]{4,3,2,0,1:T(8,128)} %get-tuple-element.17), channel_id=1, source_target_pairs={{4,0},{8,4},{12,8},{16,12},{20,16},{24,20},{28,24},{0,28},{5,1},{9... | collective-permute-start | bytes 1179656 | tf_op jit(solution)/shard_map/ppermute | solution.py:21
  12.3 13.0 %collective-permute-start.5 = (f32[32,3,1,8,128]{4,3,2,0,1:T(8,128)}, f32[32,3,1,8,128]{4,3,2,0,1:T(8,128)}, u32[]{:S(2)}, u32[]{:S(2)}) collective-permute-start(f32[32,3,1,8,128]{4,3,2,0,1:T(8,128)} %get-tuple-element.18), channel_id=1, source_target_pairs={{0,4},{4,8},{8,12},{12,16},{16,20},{20,24},{24,28},{28,0},{1,5},{5... | collective-permute-start | bytes 1179656 | tf_op jit(solution)/shard_map/ppermute | solution.py:20
  18.5 4.8 %collective-permute-start.2 = (f32[3,8,2,128]{3,2,1,0:T(2,128)S(1)}, f32[3,8,2,128]{3,2,1,0:T(2,128)S(1)}, u32[]{:S(2)}, u32[]{:S(2)}) collective-permute-start(f32[3,8,2,128]{3,2,1,0:T(2,128)S(1)} %get-tuple-element.47), channel_id=1, source_target_pairs={{0,1},{1,2},{2,3},{3,0},{4,5},{5,6},{6,7},{7,4},{8,9},{9,10},{10,1... | collective-permute-start | bytes 73736 | tf_op jit(solution)/shard_map/ppermute | solution.py:20
  20.1 3.8 %collective-permute-start.3 = (f32[3,8,2,128]{3,2,1,0:T(2,128)S(1)}, f32[3,8,2,128]{3,2,1,0:T(2,128)S(1)}, u32[]{:S(2)}, u32[]{:S(2)}) collective-permute-start(f32[3,8,2,128]{3,2,1,0:T(2,128)S(1)} %get-tuple-element.48), channel_id=1, source_target_pairs={{1,0},{2,1},{3,2},{0,3},{5,4},{6,5},{7,6},{4,7},{9,8},{10,9},{11,1... | collective-permute-start | bytes 73736 | tf_op jit(solution)/shard_map/ppermute | solution.py:21
  27.1 9.0 %collective-permute-start.7 = (f32[32,3,6,1,128]{4,0,3,2,1:T(8,128)S(1)}, f32[32,3,6,1,128]{4,0,3,2,1:T(8,128)S(1)}, u32[]{:S(2)}, u32[]{:S(2)}) collective-permute-start(f32[32,3,6,1,128]{4,0,3,2,1:T(8,128)S(1)} %copy.59), channel_id=1, source_target_pairs={{0,1},{1,2},{2,3},{3,0},{4,5},{5,6},{6,7},{7,4},{8,9},{9,10},{10,1... | collective-permute-start | bytes 884744 | tf_op jit(solution)/shard_map/ppermute | solution.py:20
  29.5 9.7 %collective-permute-start.6 = (f32[32,3,6,1,128]{4,0,3,2,1:T(8,128)S(1)}, f32[32,3,6,1,128]{4,0,3,2,1:T(8,128)S(1)}, u32[]{:S(2)}, u32[]{:S(2)}) collective-permute-start(f32[32,3,6,1,128]{4,0,3,2,1:T(8,128)S(1)} %copy.57), channel_id=1, source_target_pairs={{1,0},{2,1},{3,2},{0,3},{5,4},{6,5},{7,6},{4,7},{9,8},{10,9},{11,1... | collective-permute-start | bytes 884744 | tf_op jit(solution)/shard_map/ppermute | solution.py:21
  30.6 8.9 %copy-start.1 = (f32[32,3,4,8,1]{4,3,2,0,1:T(8,128)S(1)}, f32[32,3,4,8,1]{4,3,2,0,1:T(8,128)}, u32[]{:S(2)}) copy-start(f32[32,3,4,8,1]{4,3,2,0,1:T(8,128)} %get-tuple-element.22) | copy-start | bytes 36868
  30.6 8.9 %copy-start.2 = (f32[32,3,4,8,127]{4,3,2,0,1:T(8,128)S(1)}, f32[32,3,4,8,127]{4,3,2,0,1:T(8,128)}, u32[]{:S(2)}) copy-start(f32[32,3,4,8,127]{4,3,2,0,1:T(8,128)} %get-tuple-element.23) | copy-start | bytes 4681732
  30.6 8.9 %copy-start.3 = (f32[32,3,4,8,127]{4,3,2,0,1:T(8,128)S(1)}, f32[32,3,4,8,127]{4,3,2,0,1:T(8,128)}, u32[]{:S(2)}) copy-start(f32[32,3,4,8,127]{4,3,2,0,1:T(8,128)} %get-tuple-element.24) | copy-start | bytes 4681732
where the time goes:
time: 100 us; the launch traced here: 99.8 us
  blocking collectives  40.7 us (41%)
  local copies, waits for them, and re-layouts  17.7 us (18%)
  starting transfers between devices  14 us (14%)
  other arithmetic  11.8 us (12%)
  waiting for transfers between devices  9.93 us (10%)
  matrix products  4.68 us (5%)
    psum x1, blocking collectives, on_device(): gram = lax.psum(partial_gram, ('gx', 'gy')) / float(entries)  40.7 us
    ppermute x4, starting transfers between devices, with_halo(): after = lax.ppermute(first, axis, down)  10 us
    unnamed x16, local copies, waits for them, and re-layouts  6.64 us
    ppermute x4, waiting for transfers between devices, with_halo(): before = lax.ppermute(last, axis, up)  6.43 us
    ppermute x4, starting transfers between devices, with_halo(): before = lax.ppermute(last, axis, up)  3.99 us
    slice x2, local copies, waits for them, and re-layouts, adjoint(): jnp.roll(inner, 1, axis=-1)  3.94 us
    slice x4, local copies, waits for them, and re-layouts, with_halo(): first = lax.slice_in_dim(value, 0, width, axis=dim)  3.93 us
    add x1, other arithmetic, adjoint(): return inner + ADVECT * (flux - coupling) + DIFFUSE * laplacian  3.88 us
  transfers between devices with their start and end apart: 8, of which 4 were waited for; matrix products, arithmetic and copies ran while one was open for 13% of the time, Pallas kernels for 0%

commit v1 on v0

--- a/solution.py
+++ b/solution.py
@@ -97,7 +97,7 @@
         flat, flat.T, precision=lax.Precision.HIGHEST, preferred_element_type=jnp.float32
     )
     entries = flat.shape[1] * lax.axis_size("gx") * lax.axis_size("gy")
-    gram = lax.psum(partial_gram, ("gx", "gy")) / float(entries)
+    gram = jnp.sum(lax.all_gather(partial_gram, ("gx", "gy")), axis=0) / float(entries)
     lower = jnp.linalg.cholesky(gram)
     inverse = lax.linalg.triangular_solve(
         lower, jnp.eye(vectors, dtype=jnp.float32), left_side=True, lower=True

time: 100 us -> 132 us (1.32)
  blocking collectives: 40.7 us -> 72.9 us
    all_gather x0 -> x1, blocking collectives: none -> 72.9 us  [on_device(): lax.all_gather(partial_gram, ('gx', 'gy'))]
    psum x1 -> x0, blocking collectives: 40.7 us -> none  [on_device(): gram = lax.psum(partial_gram, ('gx', 'gy')) / float(entries)]
  transfers between devices with their start and end apart: 8 -> 8, of which waited for: 4 -> 4; matrix products, arithmetic and copies ran while one was open for 13% -> 9% of each run, Pallas kernels for 0% -> 0%
where the time goes in v1:
time: 132 us
  blocking collectives  72.9 us (55%)
  local copies, waits for them, and re-layouts  17.7 us (13%)
  starting transfers between devices  14 us (11%)
  other arithmetic  11.9 us (9%)
  waiting for transfers between devices  9.93 us (8%)
  matrix products  4.67 us (4%)
    all_gather x1, blocking collectives, on_device(): lax.all_gather(partial_gram, ('gx', 'gy'))  72.9 us
    ppermute x4, starting transfers between devices, with_halo(): after = lax.ppermute(first, axis, down)  10 us
    unnamed x16, local copies, waits for them, and re-layouts  6.64 us
    ppermute x4, waiting for transfers between devices, with_halo(): before = lax.ppermute(last, axis, up)  6.43 us
    ppermute x4, starting transfers between devices, with_halo(): before = lax.ppermute(last, axis, up)  3.99 us
    slice x2, local copies, waits for them, and re-layouts, adjoint(): jnp.roll(inner, 1, axis=-1)  3.94 us
    slice x4, local copies, waits for them, and re-layouts, with_halo(): first = lax.slice_in_dim(value, 0, width, axis=dim)  3.93 us
    add x1, other arithmetic, adjoint(): return inner + ADVECT * (flux - coupling) + DIFFUSE * laplacian  3.88 us
  transfers between devices with their start and end apart: 8, of which 4 were waited for; matrix products, arithmetic and copies ran while one was open for 9% of the time, Pallas kernels for 0%

profile of v1, /device:TPU:0, one launch (start us, length us, event | category | flops | bytes accessed | tf_op | source)
XLA Modules:
  0.0 132.0 jit_solution(6391240261035136257)
XLA Ops:
  0.6 1.5 %fusion.34 = (f32[3,2,8,128]{3,2,1,0:T(8,128)}, f32[3,2,8,128]{3,2,1,0:T(8,128)}) fusion(f32[3,4,8,128]{3,2,1,0:T(8,128)} %param.2), kind=kLoop, calls=%fused_computation.78 | loop fusion | bytes 98304 | tf_op jit(solution)/shard_map/slice | solution.py:19
  2.1 4.5 %collective-permute-start.1 = (f32[3,2,8,128]{3,2,1,0:T(8,128)}, f32[3,2,8,128]{3,2,1,0:T(8,128)}, u32[]{:S(2)}, u32[]{:S(2)}) collective-permute-start(f32[3,2,8,128]{3,2,1,0:T(8,128)} %get-tuple-element.49), channel_id=1, source_target_pairs={{4,0},{8,4},{12,8},{16,12},{20,16},{24,20},{28,24},{0,28},{5,1},{9... | collective-permute-start | bytes 73736 | tf_op jit(solution)/shard_map/ppermute | solution.py:21
  6.7 2.1 %fusion.24 = (f32[32,3,1,8,128]{4,3,2,0,1:T(8,128)}, f32[32,3,1,8,128]{4,3,2,0,1:T(8,128)}) fusion(f32[32,3,4,8,128]{4,3,2,1,0:T(8,128)} %param.3), kind=kLoop, calls=%fused_computation.68 | loop fusion | bytes 1572864 | tf_op jit(solution)/shard_map/slice | solution.py:19
  8.7 3.5 %collective-permute-start.4 = (f32[32,3,1,8,128]{4,3,2,0,1:T(8,128)}, f32[32,3,1,8,128]{4,3,2,0,1:T(8,128)S(1)}, u32[]{:S(2)}, u32[]{:S(2)}) collective-permute-start(f32[32,3,1,8,128]{4,3,2,0,1:T(8,128)} %get-tuple-element.17), channel_id=1, source_target_pairs={{4,0},{8,4},{12,8},{16,12},{20,16},{24,20},{28,24},{0,28},{5,1},{9... | collective-permute-start | bytes 1179656 | tf_op jit(solution)/shard_map/ppermute | solution.py:21
  12.3 1.7 %fusion.25 = (f32[32,3,4,8,1]{4,3,2,0,1:T(8,128)S(1)}, f32[32,3,4,8,1]{4,3,2,0,1:T(8,128)}) fusion(f32[32,3,4,8,128]{4,3,2,1,0:T(8,128)S(1)} %copy-done), kind=kLoop, calls=%fused_computation.69 | loop fusion | bytes 3170304 | tf_op jit(solution)/shard_map/jit(_roll_static)/slice | solution.py:79
  14.0 2.2 %fusion.26 = (f32[32,3,4,8,127]{4,3,2,0,1:T(8,128)}, f32[32,3,4,8,127]{4,3,2,0,1:T(8,128)}) fusion(f32[32,3,4,8,128]{4,3,2,1,0:T(8,128)S(1)} %copy-done), kind=kLoop, calls=%fused_computation.70 | loop fusion | bytes 6266880 | tf_op jit(solution)/shard_map/jit(_roll_static)/slice | solution.py:79
  16.2 0.7 constant_dynamic-update-slice_fusion.2
  16.9 0.8 constant_dynamic-update-slice_fusion.1
  17.8 0.7 constant_dynamic-update-slice_fusion
  18.5 1.5 %collective-permute-start.2 = (f32[3,8,2,128]{3,2,1,0:T(2,128)S(1)}, f32[3,8,2,128]{3,2,1,0:T(2,128)S(1)}, u32[]{:S(2)}, u32[]{:S(2)}) collective-permute-start(f32[3,8,2,128]{3,2,1,0:T(2,128)S(1)} %get-tuple-element.47), channel_id=1, source_target_pairs={{0,1},{1,2},{2,3},{3,0},{4,5},{5,6},{6,7},{7,4},{8,9},{9,10},{10,1... | collective-permute-start | bytes 73736 | tf_op jit(solution)/shard_map/ppermute | solution.py:20
  20.1 1.4 %collective-permute-start.3 = (f32[3,8,2,128]{3,2,1,0:T(2,128)S(1)}, f32[3,8,2,128]{3,2,1,0:T(2,128)S(1)}, u32[]{:S(2)}, u32[]{:S(2)}) collective-permute-start(f32[3,8,2,128]{3,2,1,0:T(2,128)S(1)} %get-tuple-element.48), channel_id=1, source_target_pairs={{1,0},{2,1},{3,2},{0,3},{5,4},{6,5},{7,6},{4,7},{9,8},{10,9},{11,1... | collective-permute-start | bytes 73736 | tf_op jit(solution)/shard_map/ppermute | solution.py:21
  21.5 0.1 copy.60
  21.7 1.6 %collective-permute-done.2 = f32[3,8,2,128]{3,2,1,0:T(2,128)S(1)} collective-permute-done((f32[3,8,2,128]{3,2,1,0:T(2,128)S(1)}, f32[3,8,2,128]{3,2,1,0:T(2,128)S(1)}, u32[]{:S(2)}, u32[]{:S(2)}) %collective-permute-start.2) | collective-permute-done | bytes 24608 | tf_op jit(solution)/shard_map/ppermute | solution.py:20
  23.3 0.6 collective-permute-done.3
  24.0 0.1 fusion.29
  24.1 0.1 fusion.30
  24.2 0.2 subtract_add_fusion
  24.4 0.1 fusion.31
  24.5 0.1 fusion.32
  24.5 0.1 slice_subtract_fusion
  24.6 0.5 multiply_reduce_fusion.2
  25.2 1.0 constant_dynamic-update-slice_fusion.5
  26.2 0.3 constant_dynamic-update-slice_fusion.4
  26.6 0.4 fusion.23
  27.1 2.4 %collective-permute-start.7 = (f32[32,3,6,1,128]{4,0,3,2,1:T(8,128)S(1)}, f32[32,3,6,1,128]{4,0,3,2,1:T(8,128)S(1)}, u32[]{:S(2)}, u32[]{:S(2)}) collective-permute-start(f32[32,3,6,1,128]{4,0,3,2,1:T(8,128)S(1)} %copy.57), channel_id=1, source_target_pairs={{0,1},{1,2},{2,3},{3,0},{4,5},{5,6},{6,7},{7,4},{8,9},{9,10},{10,1... | collective-permute-start | bytes 884744 | tf_op jit(solution)/shard_map/ppermute | solution.py:20
  29.5 0.5 collective-permute-start.6
  30.0 0.6 fusion.28
  30.6 0.6 fusion.27
  31.2 4.8 %collective-permute-done.7 = f32[32,3,6,1,128]{4,0,3,2,1:T(8,128)S(1)} collective-permute-done((f32[32,3,6,1,128]{4,0,3,2,1:T(8,128)S(1)}, f32[32,3,6,1,128]{4,0,3,2,1:T(8,128)S(1)}, u32[]{:S(2)}, u32[]{:S(2)}) %collective-permute-start.7) | collective-permute-done | bytes 294944 | tf_op jit(solution)/shard_map/ppermute | solution.py:20
  36.0 0.3 copy.58
  36.3 2.9 %collective-permute-done.6 = f32[32,3,6,1,128]{4,0,3,2,1:T(8,128)S(1)} collective-permute-done((f32[32,3,6,1,128]{4,0,3,2,1:T(8,128)S(1)}, f32[32,3,6,1,128]{4,0,3,2,1:T(8,128)S(1)}, u32[]{:S(2)}, u32[]{:S(2)}) %collective-permute-start.6) | collective-permute-done | bytes 294944 | tf_op jit(solution)/shard_map/ppermute | solution.py:21
  39.2 0.3 copy.56
  39.6 3.9 %fusion.4 = f32[32,3,4,8,128]{4,3,2,0,1:T(8,128)S(1)} fusion(f32[32,3,4,8,128]{4,3,2,0,1:T(8,128)S(1)} %copy.60, f32[32,3,4,8,1]{4,3,2,0,1:T(8,128)S(1)} %get-tuple-element.26, f32[32,3,4,8,127]{4,3,2,0,1:T(8,128)S(1)} %get-tuple-element.28, f32[32,3,4,8,127]{4,3,2,0,1:T(8,128)S(1)} %get-tuple-element.27, f32[32,3,4,8,1]{4,3,2,0,1:T(8,128)S(1)} %get-tuple-element.25, ...), kind=kLoop, calls=%fused_computation.10 | loop fusion | flops 12189696 | bytes 14811136 | tf_op jit(solution)/shard_map/add | solution.py:82
  43.5 2.2 %fusion.12 = f32[32,32]{1,0:T(8,128)S(1)} fusion(f32[32,3,4,8,128]{4,3,2,0,1:T(8,128)S(1)} %fusion.4), kind=kOutput, calls=%fused_computation.22 | convolution fusion | flops 150994944 | bytes 1576960 | tf_op jit(solution)/shard_map/dot_general | solution.py:96
  45.6 0.1 copy.70
  45.8 0.9 copy.93
  46.7 0.3 copy.77
  47.0 72.9 %all-gather = f32[1024,32]{1,0:T(8,128)S(1)} all-gather(f32[32,32]{1,0:T(8,128)S(1)} %fusion.12), channel_id=2, replica_groups=mesh['gx'=8,'gy'=4] {'gx','gy'}, dimensions={0}, use_global_device_ids=true | all-gather | bytes 135168 | tf_op jit(solution)/shard_map/all_gather | solution.py:100
  119.9 0.1 copy.68
  120.0 0.1 copy.69
  120.1 2.9 %cholesky.17 = f32[32,32]{1,0:T(8,128)S(1)} custom-call(f32[32,32]{1,0:T(8,128)S(1)} %fusion.16), custom_call_target="Cholesky" | custom-call | tf_op jit(solution)/shard_map/jit(cholesky)/cholesky | solution.py:101
  123.0 0.6 compare_reduce_fusion
  123.7 0.7 fusion.17
  124.3 0.7 copy.73
  125.0 2.4 %custom-call.6 = f32[1,32,32]{1,2,0:T(8,128)S(1)} custom-call(f32[1,32,32]{2,1,0:T(8,128)S(1)} %get-tuple-element.52), custom_call_target="InvertDiagBlocksLowerTriangular" | custom-call | tf_op jit(solution)/shard_map/triangular_solve | solution.py:102
  127.4 0.2 convolution_bitcast_fusion
  127.7 2.3 %fusion.8 = f32[32,3,4,8,128]{4,0,3,2,1:T(8,128)S(1)} fusion(f32[32,32,1,1,1]{1,0,4,3,2:T(8,128)S(1)} %convolution_bitcast_fusion, f32[3,4,8,128,32]{3,2,1,0,4:T(8,128)S(1)} %bitcast.53), kind=kOutput, calls=%fused_computation.15 | convolution fusion | flops 150994944 | bytes 3149824 | tf_op jit(solution)/shard_map/dot_general | solution.py:105
  130.0 2.1 %copy.72 = f32[32,3,4,8,128]{4,3,2,1,0:T(8,128)} copy(f32[32,3,4,8,128]{4,0,3,2,1:T(8,128)S(1)} %fusion.8) | data formatting | bytes 3145728
  (27 shorter events, 0.4 us)
Async XLA Ops:
  0.6 11.6 %copy-start = (f32[32,3,4,8,128]{4,3,2,1,0:T(8,128)S(1)}, f32[32,3,4,8,128]{4,3,2,1,0:T(8,128)}, u32[]{:S(2)}) copy-start(f32[32,3,4,8,128]{4,3,2,1,0:T(8,128)} %param.3) | copy-start | bytes 4718596
  2.1 15.6 %collective-permute-start.1 = (f32[3,2,8,128]{3,2,1,0:T(8,128)}, f32[3,2,8,128]{3,2,1,0:T(8,128)}, u32[]{:S(2)}, u32[]{:S(2)}) collective-permute-start(f32[3,2,8,128]{3,2,1,0:T(8,128)} %get-tuple-element.49), channel_id=1, source_target_pairs={{4,0},{8,4},{12,8},{16,12},{20,16},{24,20},{28,24},{0,28},{5,1},{9... | collective-permute-start | bytes 73736 | tf_op jit(solution)/shard_map/ppermute | solution.py:21
  6.7 9.6 %collective-permute-start = (f32[3,2,8,128]{3,2,1,0:T(8,128)}, f32[3,2,8,128]{3,2,1,0:T(8,128)}, u32[]{:S(2)}, u32[]{:S(2)}) collective-permute-start(f32[3,2,8,128]{3,2,1,0:T(8,128)} %get-tuple-element.50), channel_id=1, source_target_pairs={{0,4},{4,8},{8,12},{12,16},{16,20},{20,24},{24,28},{28,0},{1,5},{5... | collective-permute-start | bytes 73736 | tf_op jit(solution)/shard_map/ppermute | solution.py:20
  8.7 17.9 %collective-permute-start.4 = (f32[32,3,1,8,128]{4,3,2,0,1:T(8,128)}, f32[32,3,1,8,128]{4,3,2,0,1:T(8,128)S(1)}, u32[]{:S(2)}, u32[]{:S(2)}) collective-permute-start(f32[32,3,1,8,128]{4,3,2,0,1:T(8,128)} %get-tuple-element.17), channel_id=1, source_target_pairs={{4,0},{8,4},{12,8},{16,12},{20,16},{24,20},{28,24},{0,28},{5,1},{9... | collective-permute-start | bytes 1179656 | tf_op jit(solution)/shard_map/ppermute | solution.py:21
  12.3 13.0 %collective-permute-start.5 = (f32[32,3,1,8,128]{4,3,2,0,1:T(8,128)}, f32[32,3,1,8,128]{4,3,2,0,1:T(8,128)}, u32[]{:S(2)}, u32[]{:S(2)}) collective-permute-start(f32[32,3,1,8,128]{4,3,2,0,1:T(8,128)} %get-tuple-element.18), channel_id=1, source_target_pairs={{0,4},{4,8},{8,12},{12,16},{16,20},{20,24},{24,28},{28,0},{1,5},{5... | collective-permute-start | bytes 1179656 | tf_op jit(solution)/shard_map/ppermute | solution.py:20
  18.5 4.8 %collective-permute-start.2 = (f32[3,8,2,128]{3,2,1,0:T(2,128)S(1)}, f32[3,8,2,128]{3,2,1,0:T(2,128)S(1)}, u32[]{:S(2)}, u32[]{:S(2)}) collective-permute-start(f32[3,8,2,128]{3,2,1,0:T(2,128)S(1)} %get-tuple-element.47), channel_id=1, source_target_pairs={{0,1},{1,2},{2,3},{3,0},{4,5},{5,6},{6,7},{7,4},{8,9},{9,10},{10,1... | collective-permute-start | bytes 73736 | tf_op jit(solution)/shard_map/ppermute | solution.py:20
  20.1 3.8 %collective-permute-start.3 = (f32[3,8,2,128]{3,2,1,0:T(2,128)S(1)}, f32[3,8,2,128]{3,2,1,0:T(2,128)S(1)}, u32[]{:S(2)}, u32[]{:S(2)}) collective-permute-start(f32[3,8,2,128]{3,2,1,0:T(2,128)S(1)} %get-tuple-element.48), channel_id=1, source_target_pairs={{1,0},{2,1},{3,2},{0,3},{5,4},{6,5},{7,6},{4,7},{9,8},{10,9},{11,1... | collective-permute-start | bytes 73736 | tf_op jit(solution)/shard_map/ppermute | solution.py:21
  27.1 9.0 %collective-permute-start.7 = (f32[32,3,6,1,128]{4,0,3,2,1:T(8,128)S(1)}, f32[32,3,6,1,128]{4,0,3,2,1:T(8,128)S(1)}, u32[]{:S(2)}, u32[]{:S(2)}) collective-permute-start(f32[32,3,6,1,128]{4,0,3,2,1:T(8,128)S(1)} %copy.57), channel_id=1, source_target_pairs={{0,1},{1,2},{2,3},{3,0},{4,5},{5,6},{6,7},{7,4},{8,9},{9,10},{10,1... | collective-permute-start | bytes 884744 | tf_op jit(solution)/shard_map/ppermute | solution.py:20
  29.5 9.7 %collective-permute-start.6 = (f32[32,3,6,1,128]{4,0,3,2,1:T(8,128)S(1)}, f32[32,3,6,1,128]{4,0,3,2,1:T(8,128)S(1)}, u32[]{:S(2)}, u32[]{:S(2)}) collective-permute-start(f32[32,3,6,1,128]{4,0,3,2,1:T(8,128)S(1)} %copy.55), channel_id=1, source_target_pairs={{1,0},{2,1},{3,2},{0,3},{5,4},{6,5},{7,6},{4,7},{9,8},{10,9},{11,1... | collective-permute-start | bytes 884744 | tf_op jit(solution)/shard_map/ppermute | solution.py:21
  30.6 8.9 %copy-start.1 = (f32[32,3,4,8,1]{4,3,2,0,1:T(8,128)S(1)}, f32[32,3,4,8,1]{4,3,2,0,1:T(8,128)}, u32[]{:S(2)}) copy-start(f32[32,3,4,8,1]{4,3,2,0,1:T(8,128)} %get-tuple-element.22) | copy-start | bytes 36868
  30.6 8.9 %copy-start.2 = (f32[32,3,4,8,127]{4,3,2,0,1:T(8,128)S(1)}, f32[32,3,4,8,127]{4,3,2,0,1:T(8,128)}, u32[]{:S(2)}) copy-start(f32[32,3,4,8,127]{4,3,2,0,1:T(8,128)} %get-tuple-element.23) | copy-start | bytes 4681732
  30.6 8.9 %copy-start.3 = (f32[32,3,4,8,127]{4,3,2,0,1:T(8,128)S(1)}, f32[32,3,4,8,127]{4,3,2,0,1:T(8,128)}, u32[]{:S(2)}) copy-start(f32[32,3,4,8,127]{4,3,2,0,1:T(8,128)} %get-tuple-element.24) | copy-start | bytes 4681732
